TPU v7x, 32 devices: a whole 2x2x4 slice. The times are simulated.
32 devices in a mesh: frame: 4 (over y, x), vox: 8 (over z, core).
Axes of the slice: x: 2, y: 2, z: 4, core: 2. Of those that a mesh axis runs over, the one named last changes fastest.
Arguments:
- pool: bfloat16 [2048, 8192], P('frame', 'vox'), may hold values from -6 to 6
- dictionary: bfloat16 [1024, 8192], P(None, 'vox'), may hold values from -0.13258252 to 0.13258252
- support: int32 [1024, 64], P(None, 'vox'), may hold values from 0 to 1, as said below
- pick: int32 [1024], P('frame'), may hold values from 0 to 511
Outputs:
- codes: bfloat16 [1024, 1024], P('frame')
- gradient: float32 [1024, 8192], P('frame', 'vox')
Inputs may be any that keep to these rules, and one draw needn't show every extreme that they name: Every mode has at least one voxel block in its support.
All inputs are finite; a program needn't handle non-finite values.
Results may differ from a plain program's by a relative error of at most 0.015.
Values may be sent and summed in bfloat16 or wider, within the bound.
No kernel may reach another device: no remote copies, remote signals or barrier semaphores. Data moves between devices by JAX's collectives and lax.ppermute only.
A program may use at most 64 MiB of HBM per device.

v0:
```python
import jax
import jax.numpy as jnp
from jax import lax
from jax.sharding import PartitionSpec as P

BLOCK = 128


def shrink(value, limit):
    return jnp.sign(value) * jnp.maximum(jnp.abs(value) - limit, 0.0)


def against(left, right):
    return lax.dot_general(
        left, right, (((1,), (1,)), ((), ())), preferred_element_type=jnp.float32
    )


def body(pool, dictionary, support, pick):
    batch = pool[pick]
    batch_wide = batch.astype(jnp.float32)
    keep = jnp.repeat(support, BLOCK, axis=1).astype(jnp.bfloat16)
    masked = dictionary * keep
    corr_local = against(batch, masked)
    energy_local = jnp.sum(jnp.square(masked.astype(jnp.float32)), axis=1)
    corr, energy = lax.psum((corr_local, energy_local), "vox")
    step = 1.0 / (energy + 1e-05)
    first = shrink(corr * step, 0.3 * step).astype(jnp.bfloat16)
    resid = (jnp.dot(first, masked, preferred_element_type=jnp.float32) - batch_wide).astype(
        jnp.bfloat16
    )
    push = lax.psum(against(resid, masked), "vox")
    codes = shrink(first.astype(jnp.float32) - step * push, 0.3 * step).astype(jnp.bfloat16)
    error = (jnp.dot(codes, masked, preferred_element_type=jnp.float32) - batch_wide).astype(
        jnp.bfloat16
    )
    groups = lax.axis_size("frame")
    own_rows = support.shape[0] // groups
    summed = lax.psum_scatter(
        lax.dot_general(
            codes, error, (((0,), (0,)), ((), ())), preferred_element_type=jnp.float32
        ).astype(jnp.bfloat16),
        "frame",
        scatter_dimension=0,
        tiled=True,
    ).astype(jnp.float32)
    keep_rows = lax.dynamic_slice_in_dim(keep, lax.axis_index("frame") * own_rows, own_rows, 0)
    gradient = keep_rows.astype(jnp.float32) * summed / (batch.shape[0] * groups)
    return (codes, gradient)


def solution(mesh):
    placed = (P("frame", "vox"), P(None, "vox"), P(None, "vox"), P("frame"))
    return jax.shard_map(
        body,
        mesh=mesh,
        in_specs=placed,
        out_specs=(P("frame", None), P("frame", "vox")),
        check_vma=False,
    )
```

profile of v0, /device:TPU:0, one launch (start us, length us, event | category | flops | bytes accessed | tf_op | source)
XLA Modules:
  0.0 196.3 jit_solution(7475399886197143005)
XLA Ops:
  7.2 0.0 copy-start
  7.2 0.0 all-reduce.3.cloned.1.call-start
  7.2 0.8 convert_element_type.37
  8.1 0.2 copy.6
  8.2 0.0 copy-start.1
  8.3 0.8 compare_select_fusion
  9.1 2.9 %broadcast_in_dim.5 = bf16[1024,8,128]{2,1,0:T(8,128)(2,1)S(1)} broadcast(bf16[1024,8]{1,0:T(8,128)(2,1)S(1)} %copy.6), dimensions={0,1} | broadcast | bytes 2113536 | tf_op jit(solution)/shard_map/broadcast_in_dim | solution.py:22
  12.0 2.1 %multiply_reduce_fusion = (f32[1024]{0:T(1024)S(1)}, bf16[1024,1024]{1,0:T(8,128)(2,1)}) fusion(bf16[1024,1024]{1,0:T(8,128)(2,1)S(1)} %copy-done.1, bf16[128,8,8,128]{3,2,1,0:T(8,128)(2,1)S(1)} %bitcast.14), kind=kLoop, calls=%fused_computation.1 | loop fusion | flops 4193280 | bytes 6295552 | tf_op jit(solution)/shard_map/reduce_sum | solution.py:25
  14.1 2.0 gather_fusion
  16.1 3.5 %fusion.5 = f32[256,1024]{1,0:T(8,128)} fusion(bf16[256,1024]{1,0:T(8,128)(2,1)} %gather_fusion, bf16[1024,1024]{1,0:T(8,128)(2,1)} %get-tuple-element.3), kind=kOutput, calls=%fused_computation.17 | convolution fusion | flops 536870912 | bytes 3670016 | tf_op jit(solution)/shard_map/dot_general | solution.py:14
  19.6 0.0 all-reduce.3.cloned.1.call-update
  19.6 0.0 all-reduce.5.cloned.1.call-start
  19.6 18.4 %psum.22 = f32[1024]{0:T(1024)S(1)} all-reduce(f32[1024]{0:T(1024)S(1)} %get-tuple-element.2), channel_id=1, replica_groups=mesh['frame'=4,'vox'=8] {'vox'}, use_global_device_ids=true, to_apply=%region_2.0 | all-reduce | flops 1024 | bytes 8192 | tf_op jit(solution)/shard_map/psum | solution.py:26
  38.1 43.5 %all-reduce.3.cloned.1.call-done = f32[256,1024]{1,0:T(8,128)} async-done(((f32[256,1024]{1,0:T(8,128)}), f32[256,1024]{1,0:T(8,128)}) %all-reduce.3.cloned.1.call-update) | async-done | bytes 1048592 | tf_op jit(solution)/shard_map/psum | solution.py:26
  81.6 5.1 %fusion.2 = f32[256,1024]{1,0:T(8,128)} fusion(bf16[1024,1024]{1,0:T(8,128)(2,1)} %get-tuple-element.3, bf16[256,1024]{1,0:T(8,128)(2,1)} %gather_fusion, f32[256,1024]{1,0:T(8,128)} %all-reduce.3.cloned.1.call-done, f32[1024]{0:T(1024)S(1)} %get-tuple-element.5, f32[1024]{0:T(1024)S(1)} %get-tuple-element.4), kind=kOutput, calls=%fused_computation.11 | convolution fusion | flops 1076363264 | bytes 4726784 | tf_op jit(solution)/shard_map/dot_general | solution.py:14
  86.7 0.0 all-reduce.5.cloned.1.call-update
  86.7 0.0 reduce-scatter.2.cloned.1.call-start
  86.8 58.4 %all-reduce.5.cloned.1.call-done = f32[256,1024]{1,0:T(8,128)} async-done(((f32[256,1024]{1,0:T(8,128)}), f32[256,1024]{1,0:T(8,128)}) %all-reduce.5.cloned.1.call-update) | async-done | bytes 1048592 | tf_op jit(solution)/shard_map/psum | solution.py:32
  145.2 3.2 %multiply_convert_fusion = bf16[256,1024]{1,0:T(8,128)(2,1)} fusion(f32[256,1024]{1,0:T(8,128)} %all-reduce.5.cloned.1.call-done, f32[1024]{0:T(1024)S(1)} %get-tuple-element.5, f32[1024]{0:T(1024)S(1)} %get-tuple-element.4, f32[256,1024]{1,0:T(8,128)} %all-reduce.3.cloned.1.call-done), kind=kLoop, calls=%fused_computation.9 | loop fusion | flops 4194304 | bytes 2629632 | tf_op jit(solution)/shard_map/convert_element_type | solution.py:33
  148.4 4.5 %convolution_convert_fusion = bf16[1024,1024]{1,0:T(8,128)(2,1)} fusion(bf16[256,1024]{1,0:T(8,128)(2,1)} %multiply_convert_fusion, bf16[256,1024]{1,0:T(8,128)(2,1)} %gather_fusion, bf16[1024,1024]{1,0:T(8,128)(2,1)} %get-tuple-element.3), kind=kOutput, calls=%fused_computation.3 | convolution fusion | flops 1075576832 | bytes 5242880 | tf_op jit(solution)/shard_map/dot_general | solution.py:40
  152.9 0.0 reduce-scatter.2.cloned.1.call-update
  153.0 2.0 %copy.12 = bf16[128,8,8,128]{3,1,2,0:T(8,128)(2,1)} copy(bf16[128,8,8,128]{3,2,1,0:T(8,128)(2,1)S(1)} %bitcast.15) | data formatting | bytes 4194304
  155.0 32.4 %reduce-scatter.2.cloned.1.call-done = bf16[256,1024]{1,0:T(8,128)(2,1)} async-done(((bf16[1024,1024]{1,0:T(8,128)(2,1)}), bf16[256,1024]{1,0:T(8,128)(2,1)}) %reduce-scatter.2.cloned.1.call-update) | async-done | bytes 524304 | tf_op jit(solution)/shard_map/reduce_scatter | solution.py:39
  187.4 2.4 %multiply_multiply_fusion = f32[256,1024]{1,0:T(8,128)} fusion(bf16[256,1024]{1,0:T(8,128)(2,1)} %reduce-scatter.2.cloned.1.call-done, bf16[1024,1024]{1,0:T(8,128)(2,1)} %bitcast.16, s32[]{:T(128)S(6)} %select_n.7), kind=kLoop, calls=%fused_computation.8 | loop fusion | flops 1048576 | bytes 2097156 | tf_op jit(solution)/shard_map/div | solution.py:48
  (4 shorter events, 0.0 us)
Async XLA Ops:
  7.2 7.0 %copy-start = (bf16[512,1024]{1,0:T(8,128)(2,1)S(1)}, bf16[512,1024]{1,0:T(8,128)(2,1)}, u32[]{:S(2)}) copy-start(bf16[512,1024]{1,0:T(8,128)(2,1)} %param.4) | copy-start | bytes 3145732
  7.2 74.4 %all-reduce.3.cloned.1.call-start = ((), (), s32[]{:S(2)}) async-start(), calls=%async_computation.1 | async-start | bytes 2097152 | tf_op jit(solution)/shard_map/psum | solution.py:26
  8.2 3.8 %copy-start.1 = (bf16[1024,1024]{1,0:T(8,128)(2,1)S(1)}, bf16[1024,1024]{1,0:T(8,128)(2,1)}, u32[]{:S(2)}) copy-start(bf16[1024,1024]{1,0:T(8,128)(2,1)} %param.5) | copy-start | bytes 6291460
  19.6 125.6 %all-reduce.5.cloned.1.call-start = ((), (), s32[]{:S(2)}) async-start(), calls=%async_computation.2 | async-start | bytes 2097152 | tf_op jit(solution)/shard_map/psum | solution.py:32
  86.7 100.6 %reduce-scatter.2.cloned.1.call-start = ((), (), s32[]{:S(2)}) async-start(), calls=%async_computation.3 | async-start | bytes 2621440 | tf_op jit(solution)/shard_map/reduce_scatter | solution.py:39
Sparse Core Ops, SparseCore 0:
  19.7 61.8 all-reduce.2
  86.9 58.2 all-reduce.4
  153.1 34.2 reduce-scatter.1
where the time goes:
time: 197 us; the launch traced here: 196 us
  waiting for transfers between devices  134 us (68%)
  blocking collectives  18.4 us (9%)
  between operations  13.8 us (7%)
  matrix products  13.1 us (7%)
  other arithmetic  9.34 us (5%)
  local copies, waits for them, and re-layouts  7.04 us (4%)
    psum x1, waiting for transfers between devices, body(): push = lax.psum(against(resid, masked), 'vox')  58.4 us
    psum x1, waiting for transfers between devices, body(): corr, energy = lax.psum((corr_local, energy_local), 'vox')  43.5 us
    reduce_scatter x1, waiting for transfers between devices, body(): lax.psum_scatter(lax.dot_general(codes, error, (((0,), (0,)), ((), ())),...  32.4 us
    psum x1, blocking collectives, body(): corr, energy = lax.psum((corr_local, energy_local), 'vox')  18.4 us
    dot_general x2, matrix products, against(): lax.dot_general(left, right, (((1,), (1,)), ((), ())), preferred_element_...  8.6 us
    dot_general x1, matrix products, body(): lax.dot_general(codes, error, (((0,), (0,)), ((), ())), preferred_element...  4.54 us
  transfers between devices with their start and end apart: 3, of which 3 were waited for; matrix products, arithmetic and copies ran while one was open for 1% of the time, Pallas kernels for 0%

commit v1 on v0

--- a/solution.py
+++ b/solution.py
@@ -4,6 +4,7 @@
 from jax.sharding import PartitionSpec as P
 
 BLOCK = 128
+prepare_plane = lambda message: jnp.sum(lax.all_gather(message, axis_name="vox"), 0)
 
 
 def shrink(value, limit):
@@ -29,7 +30,7 @@
     resid = (jnp.dot(first, masked, preferred_element_type=jnp.float32) - batch_wide).astype(
         jnp.bfloat16
     )
-    push = lax.psum(against(resid, masked), "vox")
+    push = prepare_plane(against(resid, masked))
     codes = shrink(first.astype(jnp.float32) - step * push, 0.3 * step).astype(jnp.bfloat16)
     error = (jnp.dot(codes, masked, preferred_element_type=jnp.float32) - batch_wide).astype(
         jnp.bfloat16

time: 197 us -> 224 us (1.14)
  waiting for transfers between devices: 134 us -> 157 us
  other arithmetic: 9.34 us -> 14.7 us
    all_gather x0 -> x1, waiting for transfers between devices: none -> 81.2 us  [lax.all_gather(message, axis_name='vox')]
    psum x1 -> x0, waiting for transfers between devices: 58.4 us -> none  [body(): push = lax.psum(against(resid, masked), 'vox')]
    reduce_sum x0 -> x1, other arithmetic: none -> 5.35 us  [jnp.sum(lax.all_gather(message, axis_name='vox'), 0)]
where the time goes in v1:
time: 224 us
  waiting for transfers between devices  157 us (70%)
  blocking collectives  18.4 us (8%)
  other arithmetic  14.7 us (7%)
  between operations  13.8 us (6%)
  matrix products  13.3 us (6%)
  local copies, waits for them, and re-layouts  6.99 us (3%)
    all_gather x1, waiting for transfers between devices, lax.all_gather(message, axis_name='vox')  81.2 us
    psum x1, waiting for transfers between devices, body(): corr, energy = lax.psum((corr_local, energy_local), 'vox')  43.5 us
    reduce_scatter x1, waiting for transfers between devices, body(): lax.psum_scatter(lax.dot_general(codes, error, (((0,), (0,)), ((), ())),...  31.9 us
    psum x1, blocking collectives, body(): corr, energy = lax.psum((corr_local, energy_local), 'vox')  18.4 us
    dot_general x2, matrix products, against(): lax.dot_general(left, right, (((1,), (1,)), ((), ())), preferred_element_...  8.66 us
    reduce_sum x1, other arithmetic, jnp.sum(lax.all_gather(message, axis_name='vox'), 0)  5.35 us
    dot_general x1, matrix products, body(): lax.dot_general(codes, error, (((0,), (0,)), ((), ())), preferred_element...  4.6 us
  transfers between devices with their start and end apart: 3, of which 3 were waited for; matrix products, arithmetic and copies ran while one was open for 1% of the time, Pallas kernels for 0%

profile of v1, /device:TPU:0, one launch (start us, length us, event | category | flops | bytes accessed | tf_op | source)
XLA Modules:
  0.0 224.0 jit_solution(7031434229714498948)
XLA Ops:
  7.2 0.0 copy-start
  7.2 0.0 all-reduce.2.cloned.1.call-start
  7.2 0.8 convert_element_type.37
  8.1 0.2 copy.6
  8.3 0.8 compare_select_fusion
  9.1 2.9 %broadcast_in_dim.5 = bf16[1024,8,128]{2,1,0:T(8,128)(2,1)S(1)} broadcast(bf16[1024,8]{1,0:T(8,128)(2,1)S(1)} %copy.6), dimensions={0,1} | broadcast | bytes 2113536 | tf_op jit(solution)/shard_map/broadcast_in_dim | solution.py:23
  12.0 2.1 multiply_reduce_fusion
  14.2 2.0 gather_fusion
  16.1 3.5 %fusion.5 = f32[256,1024]{1,0:T(8,128)} fusion(bf16[256,1024]{1,0:T(8,128)(2,1)} %gather_fusion, bf16[1024,1024]{1,0:T(8,128)(2,1)} %get-tuple-element.3), kind=kOutput, calls=%fused_computation.17 | convolution fusion | flops 536870912 | bytes 3670016 | tf_op jit(solution)/shard_map/dot_general | solution.py:15
  19.6 0.0 all-reduce.2.cloned.1.call-update
  19.6 0.0 all-gather.3.cloned.1.call-start
  19.7 18.4 %psum.15 = f32[1024]{0:T(1024)S(1)} all-reduce(f32[1024]{0:T(1024)S(1)} %get-tuple-element.2), channel_id=1, replica_groups=mesh['frame'=4,'vox'=8] {'vox'}, use_global_device_ids=true, to_apply=%region_2.0 | all-reduce | flops 1024 | bytes 8192 | tf_op jit(solution)/shard_map/psum | solution.py:27
  38.1 43.5 %all-reduce.2.cloned.1.call-done = f32[256,1024]{1,0:T(8,128)} async-done(((f32[256,1024]{1,0:T(8,128)}), f32[256,1024]{1,0:T(8,128)}) %all-reduce.2.cloned.1.call-update) | async-done | bytes 1048592 | tf_op jit(solution)/shard_map/psum | solution.py:27
  81.6 5.2 %fusion.2 = f32[256,1024]{1,0:T(8,128)} fusion(bf16[1024,1024]{1,0:T(8,128)(2,1)} %get-tuple-element.3, bf16[256,1024]{1,0:T(8,128)(2,1)} %gather_fusion, f32[256,1024]{1,0:T(8,128)} %all-reduce.2.cloned.1.call-done, f32[1024]{0:T(1024)S(1)} %get-tuple-element.5, f32[1024]{0:T(1024)S(1)} %get-tuple-element.4), kind=kOutput, calls=%fused_computation.11 | convolution fusion | flops 1076363264 | bytes 4726784 | tf_op jit(solution)/shard_map/dot_general | solution.py:15
  86.8 0.0 all-gather.3.cloned.1.call-update
  86.8 0.0 reduce-scatter.2.cloned.1.call-start
  86.9 81.2 %all-gather.3.cloned.1.call-done = f32[2048,1024]{1,0:T(8,128)} async-done(((f32[256,1024]{1,0:T(8,128)}), f32[2048,1024]{1,0:T(8,128)}) %all-gather.3.cloned.1.call-update) | async-done | bytes 8388624 | tf_op jit(solution)/shard_map/all_gather | solution.py:7
  168.1 5.3 %reduce_sum.19 = f32[256,1024]{1,0:T(8,128)} reduce(f32[8,256,1024]{2,1,0:T(8,128)} %bitcast.17, f32[]{:T(128)} %constant.3.clone.1), dimensions={0}, to_apply=%region_3.0 | reduce | flops 1835008 | bytes 9437188 | tf_op jit(solution)/shard_map/reduce_sum | solution.py:7
  173.4 3.2 %multiply_convert_fusion = bf16[256,1024]{1,0:T(8,128)(2,1)} fusion(f32[256,1024]{1,0:T(8,128)} %reduce_sum.19, f32[1024]{0:T(1024)S(1)} %get-tuple-element.5, f32[1024]{0:T(1024)S(1)} %get-tuple-element.4, f32[256,1024]{1,0:T(8,128)} %all-reduce.2.cloned.1.call-done), kind=kLoop, calls=%fused_computation.9 | loop fusion | flops 4194304 | bytes 2629632 | tf_op jit(solution)/shard_map/convert_element_type | solution.py:34
  176.6 4.6 %convolution_convert_fusion = bf16[1024,1024]{1,0:T(8,128)(2,1)} fusion(bf16[256,1024]{1,0:T(8,128)(2,1)} %multiply_convert_fusion, bf16[256,1024]{1,0:T(8,128)(2,1)} %gather_fusion, bf16[1024,1024]{1,0:T(8,128)(2,1)} %get-tuple-element.3), kind=kOutput, calls=%fused_computation.3 | convolution fusion | flops 1075576832 | bytes 5242880 | tf_op jit(solution)/shard_map/dot_general | solution.py:41
  181.2 0.0 reduce-scatter.2.cloned.1.call-update
  181.2 1.9 copy.12
  183.2 31.9 %reduce-scatter.2.cloned.1.call-done = bf16[256,1024]{1,0:T(8,128)(2,1)} async-done(((bf16[1024,1024]{1,0:T(8,128)(2,1)}), bf16[256,1024]{1,0:T(8,128)(2,1)}) %reduce-scatter.2.cloned.1.call-update) | async-done | bytes 524304 | tf_op jit(solution)/shard_map/reduce_scatter | solution.py:40
  215.1 2.4 %multiply_multiply_fusion = f32[256,1024]{1,0:T(8,128)} fusion(bf16[256,1024]{1,0:T(8,128)(2,1)} %reduce-scatter.2.cloned.1.call-done, bf16[1024,1024]{1,0:T(8,128)(2,1)} %bitcast.18, s32[]{:T(128)S(6)} %select_n.7), kind=kLoop, calls=%fused_computation.8 | loop fusion | flops 1048576 | bytes 2097156 | tf_op jit(solution)/shard_map/div | solution.py:49
  (5 shorter events, 0.0 us)
Async XLA Ops:
  7.2 7.0 %copy-start = (bf16[512,1024]{1,0:T(8,128)(2,1)S(1)}, bf16[512,1024]{1,0:T(8,128)(2,1)}, u32[]{:S(2)}) copy-start(bf16[512,1024]{1,0:T(8,128)(2,1)} %param.4) | copy-start | bytes 3145732
  7.2 74.4 %all-reduce.2.cloned.1.call-start = ((), (), s32[]{:S(2)}) async-start(), calls=%async_computation.1 | async-start | bytes 2097152 | tf_op jit(solution)/shard_map/psum | solution.py:27
  8.2 3.8 %copy-start.1 = (bf16[1024,1024]{1,0:T(8,128)(2,1)S(1)}, bf16[1024,1024]{1,0:T(8,128)(2,1)}, u32[]{:S(2)}) copy-start(bf16[1024,1024]{1,0:T(8,128)(2,1)} %param.5) | copy-start | bytes 6291460
  19.6 148.4 %all-gather.3.cloned.1.call-start = ((), (), s32[]{:S(2)}) async-start(), calls=%async_computation.3 | async-start | bytes 9437184 | tf_op jit(solution)/shard_map/all_gather | solution.py:7
  86.8 128.3 %reduce-scatter.2.cloned.1.call-start = ((), (), s32[]{:S(2)}) async-start(), calls=%async_computation.2 | async-start | bytes 2621440 | tf_op jit(solution)/shard_map/reduce_scatter | solution.py:40
Sparse Core Ops, SparseCore 0:
  19.8 61.8 all-reduce.1
  86.9 81.0 all-gather.2
  181.4 33.6 reduce-scatter.1
